TPU v7x, 32 devices: a whole 2x2x4 slice. The times are simulated.
32 devices in a mesh: ctx: 8 (over y, x, core), exp: 4 (over z).
Axes of the slice: x: 2, y: 2, z: 4, core: 2. Of those that a mesh axis runs over, the one named last changes fastest.
Arguments:
- queries: bfloat16 [4096, 4096], P(('ctx', 'exp')), may hold values from -100 to 100
- keys: bfloat16 [4096, 1024], P(('ctx', 'exp')), may hold values from -100 to 100
- values: bfloat16 [4096, 1024], P(('ctx', 'exp')), may hold values from -6 to 6
- doc_ids: int32 [4096], P(('ctx', 'exp')), may hold values from 0 to 7, never falling along the last dimension, each value on 1 to 1024 neighbouring positions
- span_ids: int32 [4096], P(('ctx', 'exp')), may hold values from 0 to 3, never falling along the last dimension, each value on 1 to 2048 neighbouring positions
Outputs:
- attended: bfloat16 [4096, 4096], P(('ctx', 'exp'))
Inputs may be any that keep to these rules, and one draw needn't show every extreme that they name: `doc_ids`: never falling; each document has 1 to 1024 positions, one exactly 1024. `span_ids`: never falling; each span has 1 to 2048 positions, one exactly 2048.
All inputs are finite; a program needn't handle non-finite values.
Results may differ from a plain program's by a relative error of at most 0.0061.
Values may be sent and summed in bfloat16 or wider, within the bound.
A program may use at most 64 MiB of HBM per device.

v0:
```python
import jax
import jax.numpy as jnp
from jax import lax
from jax.sharding import PartitionSpec as P

QUERY_HEADS = 32
KEY_VALUE_HEADS = 8
HEAD_SIZE = 128
SPAN = 8192
DOC_LEN = 2048


def shifted(block, axis, distance):
    devices = range(lax.axis_size(axis))
    route = [(i - distance, i) for i in devices if i - distance in devices]
    return lax.ppermute(block, axis, route)


def single_unit_rows(tensor):
    widened = tensor.astype(jnp.float32)
    factor = lax.rsqrt(jnp.mean(widened * widened, axis=-1, keepdims=True) + 1e-06)
    return (widened * factor).astype(jnp.bfloat16)


def per_device(queries, keys, values, doc_ids, span_ids):
    expanded_size = lax.axis_size("exp")
    ctx_size = lax.axis_size("ctx")
    shard_rows = queries.shape[0]
    shard_len = shard_rows * expanded_size
    query_heads = single_unit_rows(queries.reshape(shard_rows, QUERY_HEADS, HEAD_SIZE))
    key_head_rows = single_unit_rows(keys.reshape(shard_rows, KEY_VALUE_HEADS, HEAD_SIZE))
    value_head_rows = values.reshape(shard_rows, KEY_VALUE_HEADS, HEAD_SIZE)
    head_replicas = max(1, expanded_size // KEY_VALUE_HEADS)
    reach_len = min(SPAN, DOC_LEN)
    steps_back = min((reach_len - 2) // shard_len + 1, ctx_size - 1)
    raw_pair = jnp.concatenate([key_head_rows, value_head_rows], axis=2)

    def spread(pair_rows):
        if head_replicas > 1:
            return jnp.repeat(pair_rows, head_replicas, axis=1)
        return pair_rows

    sources = []
    paired = spread(raw_pair)
    query_local, pair_local = (
        lax.all_to_all(query_heads, "exp", split_axis=1, concat_axis=0, tiled=True),
        lax.all_to_all(paired, "exp", split_axis=1, concat_axis=0, tiled=True),
    )
    block_doc, block_span = (
        lax.all_gather(doc_ids, "exp", axis=0, tiled=True),
        lax.all_gather(span_ids, "exp", axis=0, tiled=True),
    )
    sources.append((0, pair_local, block_doc, block_span))
    for distance in range(1, steps_back + 1):
        moved = shifted(pair_local, "ctx", distance)
        moved_doc, moved_span = shifted((block_doc, block_span), "ctx", distance)
        sources.append((distance, moved, moved_doc, moved_span))
    block_doc = sources[0][2]
    block_span = sources[0][3]
    local_heads = query_local.shape[1]
    pair_heads = sources[0][1].shape[1]
    query_group_width = local_heads // pair_heads
    ctx_index = lax.axis_index("ctx")
    tile_length = min(512, shard_len)
    tiles_side = shard_len // tile_length
    query_start = ctx_index * shard_len
    grouped = query_local.reshape(shard_len, pair_heads, query_group_width, HEAD_SIZE)
    inv_root = HEAD_SIZE ** (-0.5)
    offsets = jnp.arange(tile_length, dtype=jnp.int32)
    query_doc_tiles = block_doc.reshape(tiles_side, tile_length)
    query_span_tiles = block_span.reshape(tiles_side, tile_length)
    numer_list = [
        jnp.zeros((tile_length, pair_heads, query_group_width, HEAD_SIZE), jnp.float32)
        for _ in range(tiles_side)
    ]
    denom_list = [
        jnp.zeros((tile_length, pair_heads, query_group_width), jnp.float32)
        for _ in range(tiles_side)
    ]
    for distance, source, key_doc, key_span in sources:
        key_start = query_start - distance * shard_len
        present = ctx_index >= distance
        key_doc_tiles = key_doc.reshape(tiles_side, tile_length)
        key_span_tiles = key_span.reshape(tiles_side, tile_length)
        live_table = (
            (key_doc_tiles[None, :, tile_length - 1] >= query_doc_tiles[:, None, 0])
            & (key_span_tiles[None, :, tile_length - 1] >= query_span_tiles[:, None, 0])
            & present
        )
        for q_block in range(tiles_side):
            for k_block in range(tiles_side):
                q_first = q_block * tile_length
                k_first = k_block * tile_length
                static_gap = distance * shard_len + q_first - k_first
                if static_gap + tile_length - 1 < 0:
                    continue
                if static_gap - (tile_length - 1) > reach_len - 1:
                    continue

                def compute(
                    inner_acc,
                    source=source,
                    key_start=key_start,
                    q_first=q_first,
                    k_first=k_first,
                    key_doc_tiles=key_doc_tiles,
                    key_span_tiles=key_span_tiles,
                    q_block=q_block,
                    k_block=k_block,
                ):
                    numer_in, denom_in = inner_acc
                    query_tile = grouped[q_first : q_first + tile_length]
                    kv_tile = source[k_first : k_first + tile_length]
                    scores = (
                        jnp.einsum(
                            "qhgd,khd->qhgk",
                            query_tile,
                            kv_tile[:, :, :HEAD_SIZE],
                            preferred_element_type=jnp.float32,
                        )
                        * inv_root
                    )
                    q_pos = query_start + q_first + offsets
                    k_pos = key_start + k_first + offsets
                    q_doc_t = query_doc_tiles[q_block]
                    q_span_t = query_span_tiles[q_block]
                    k_doc_t = key_doc_tiles[k_block]
                    k_span_t = key_span_tiles[k_block]
                    allowed = (
                        (q_doc_t[:, None] == k_doc_t[None, :])
                        & (q_span_t[:, None] == k_span_t[None, :])
                        & (k_pos[None, :] <= q_pos[:, None])
                    )
                    weights = jnp.where(allowed[:, None, None, :], jnp.exp(scores), 0.0)
                    part_den = jnp.sum(weights, axis=3)
                    part_num = jnp.einsum(
                        "qhgk,khd->qhgd",
                        weights.astype(jnp.bfloat16),
                        kv_tile[:, :, HEAD_SIZE:],
                        preferred_element_type=jnp.float32,
                    )
                    return (numer_in + part_num, denom_in + part_den)

                numer_list[q_block], denom_list[q_block] = lax.cond(
                    live_table[q_block, k_block],
                    compute,
                    lambda inner_acc: inner_acc,
                    (numer_list[q_block], denom_list[q_block]),
                )
    numerator = jnp.concatenate(numer_list, axis=0)
    denominator = jnp.concatenate(denom_list, axis=0)
    attended = (
        (numerator / denominator[..., None])
        .astype(jnp.bfloat16)
        .reshape(shard_len, local_heads, HEAD_SIZE)
    )
    returned = lax.all_to_all(attended, "exp", split_axis=0, concat_axis=1, tiled=True)
    return returned.reshape(shard_rows, QUERY_HEADS * HEAD_SIZE)


def solution(mesh):
    in_specs = (
        P(("ctx", "exp"), None),
        P(("ctx", "exp"), None),
        P(("ctx", "exp"), None),
        P(("ctx", "exp")),
        P(("ctx", "exp")),
    )
    out_specs = P(("ctx", "exp"), None)
    return jax.shard_map(
        per_device, mesh=mesh, in_specs=in_specs, out_specs=out_specs, check_vma=False
    )
```

profile of v0, /device:TPU:6, one launch (start us, length us, event | category | flops | bytes accessed | tf_op | source)
XLA Modules:
  0.0 159.9 jit_solution(7559101673768642415)
XLA Ops:
  3.3 4.9 %all-to-all-start = ((bf16[128,8,256]{0,2,1:T(8,128)(2,1)}), bf16[128,8,256]{0,2,1:T(8,128)(2,1)S(1)}, u32[]{:S(2)}, u32[]{:S(2)}) async-start(bf16[128,8,256]{0,2,1:T(8,128)(2,1)} %pad_maximum_fusion), calls=%async_computation | async-start | bytes 1048576 | tf_op jit(solution)/shard_map/all_to_all | solution.py:47
  8.1 1.6 %copy.59 = bf16[128,4096]{0,1:T(8,128)(2,1)S(1)} copy(bf16[128,4096]{1,0:T(8,128)(2,1)} %param.15) | data formatting | bytes 2097152 | tf_op args[0]
  10.4 1.3 copy.60
  11.7 11.0 %all-to-all-done = bf16[128,8,256]{0,2,1:T(8,128)(2,1)S(1)} async-done(((bf16[128,8,256]{0,2,1:T(8,128)(2,1)}), bf16[128,8,256]{0,2,1:T(8,128)(2,1)S(1)}, u32[]{:S(2)}, u32[]{:S(2)}) %all-to-all-start) | async-done | bytes 524320 | tf_op jit(solution)/shard_map/all_to_all | solution.py:47
  22.6 3.5 %all-to-all-start.1 = ((bf16[128,32,128]{2,0,1:T(8,128)(2,1)}), bf16[128,32,128]{2,0,1:T(8,128)(2,1)S(1)}, u32[]{:S(2)}, u32[]{:S(2)}) async-start(bf16[128,32,128]{2,0,1:T(8,128)(2,1)} %copy.60), calls=%async_computation.1 | async-start | bytes 2097152 | tf_op jit(solution)/shard_map/all_to_all | solution.py:46
  27.2 1.9 %collective-permute-start.8 = (bf16[512,2,256]{2,0,1:T(8,128)(2,1)}, bf16[512,2,256]{2,0,1:T(8,128)(2,1)}, u32[]{:S(2)}, u32[]{:S(2)}) collective-permute-start(bf16[512,2,256]{2,0,1:T(8,128)(2,1)} %bitcast.60), channel_id=1, source_target_pairs={{0,4},{4,8},{8,12},{12,16},{16,20},{20,24},{24,28},{1,5},{5,9},{9,... | collective-permute-start | bytes 1572872 | tf_op jit(solution)/shard_map/ppermute | solution.py:16
  29.1 1.3 collective-permute-start.9
  30.4 1.3 collective-permute-start.10
  31.7 1.3 collective-permute-start.11
  33.0 15.6 %all-gather = s32[4,1,128]{2,1,0:T(1,128)S(1)} all-gather(s32[1,1,128]{2,1,0:T(1,128)S(1)} %bitcast.205), channel_id=1, replica_groups=mesh['ctx'=8,'exp'=4] {'exp'}, dimensions={0}, use_global_device_ids=true | all-gather | bytes 2560 | tf_op jit(solution)/shard_map/all_gather | solution.py:50
  48.6 1.9 %collective-permute-start.6 = (s32[512]{0:T(512)S(1)}, s32[512]{0:T(512)S(1)}, u32[]{:S(2)}, u32[]{:S(2)}) collective-permute-start(s32[512]{0:T(512)S(1)} %bitcast.177), channel_id=1, source_target_pairs={{0,4},{4,8},{8,12},{12,16},{16,20},{20,24},{24,28},{1,5},{5,9},{9,... | collective-permute-start | bytes 6152 | tf_op jit(solution)/shard_map/ppermute | solution.py:16
  50.6 13.9 %all-gather.1 = s32[4,1,128]{2,1,0:T(1,128)S(1)} all-gather(s32[1,1,128]{2,1,0:T(1,128)S(1)} %bitcast.206), channel_id=1, replica_groups=mesh['ctx'=8,'exp'=4] {'exp'}, dimensions={0}, use_global_device_ids=true | all-gather | bytes 2560 | tf_op jit(solution)/shard_map/all_gather | solution.py:51
  64.5 1.9 %collective-permute-start.7 = (s32[512]{0:T(512)S(1)}, s32[512]{0:T(512)S(1)}, u32[]{:S(2)}, u32[]{:S(2)}) collective-permute-start(s32[512]{0:T(512)S(1)} %bitcast.187), channel_id=1, source_target_pairs={{0,4},{4,8},{8,12},{12,16},{16,20},{20,24},{24,28},{1,5},{5,9},{9,... | collective-permute-start | bytes 6152 | tf_op jit(solution)/shard_map/ppermute | solution.py:16
  66.4 3.0 %collective-permute-done.7 = s32[512]{0:T(512)S(1)} collective-permute-done((s32[512]{0:T(512)S(1)}, s32[512]{0:T(512)S(1)}, u32[]{:S(2)}, u32[]{:S(2)}) %collective-permute-start.7) | collective-permute-done | bytes 2080 | tf_op jit(solution)/shard_map/ppermute | solution.py:16
  69.4 1.3 collective-permute-start.4
  70.7 4.2 %collective-permute-done.4 = s32[512]{0:T(512)S(1)} collective-permute-done((s32[512]{0:T(512)S(1)}, s32[512]{0:T(512)S(1)}, u32[]{:S(2)}, u32[]{:S(2)}) %collective-permute-start.4) | collective-permute-done | bytes 2080 | tf_op jit(solution)/shard_map/ppermute | solution.py:16
  74.9 1.3 collective-permute-start.5
  76.1 4.6 %collective-permute-done.5 = s32[512]{0:T(512)S(1)} collective-permute-done((s32[512]{0:T(512)S(1)}, s32[512]{0:T(512)S(1)}, u32[]{:S(2)}, u32[]{:S(2)}) %collective-permute-start.5) | collective-permute-done | bytes 2080 | tf_op jit(solution)/shard_map/ppermute | solution.py:16
  80.7 1.3 collective-permute-start.2
  82.0 3.6 %collective-permute-done.2 = s32[512]{0:T(512)S(1)} collective-permute-done((s32[512]{0:T(512)S(1)}, s32[512]{0:T(512)S(1)}, u32[]{:S(2)}, u32[]{:S(2)}) %collective-permute-start.2) | collective-permute-done | bytes 2080 | tf_op jit(solution)/shard_map/ppermute | solution.py:16
  85.6 1.3 collective-permute-start.3
  87.5 3.0 %collective-permute-done.3 = s32[512]{0:T(512)S(1)} collective-permute-done((s32[512]{0:T(512)S(1)}, s32[512]{0:T(512)S(1)}, u32[]{:S(2)}, u32[]{:S(2)}) %collective-permute-start.3) | collective-permute-done | bytes 2080 | tf_op jit(solution)/shard_map/ppermute | solution.py:16
  90.5 1.3 collective-permute-start.1
  96.0 1.3 collective-permute-start
  112.9 6.7 %conditional.5 = (f32[512,2,4,128]{3,0,2,1:T(8,128)S(1)}, f32[512,2,4]{0,2,1:T(4,128)S(1)}) conditional(s32[]{:T(128)} %bitcast.53, () %tuple.40, (s32[512]{0:T(512)S(1)}, s32[512]{0:T(512)S(1)}, s32[]{:T(128)}, s32[512]{0:T(512)S(1)}, bf16[512,2,256]{2,0,1:T(8,128)(2,1)}, /*index=5*/bf16[512,2,4,128]{3,0,2,1:T(8,128)(2,1)S(1)}) %tuple.91), branch_computations={%region_2.0_spmd, %region_3.5_spmd} | conditional | flops 1087631872 | bytes 21260308 | solution.py:144
  113.3 3.1 %fusion = (f32[512,2,4]{0,2,1:T(4,128)S(1)}, f32[2,512,512,4]{2,1,3,0:T(8,128)S(1)}) fusion(pred[512,512]{0,1:T(8,128)(4,1)S(1)} %compare_and_fusion, bf16[512,2,4,128]{3,0,2,1:T(8,128)(2,1)S(1)} %get-tuple-element.153, bf16[512,2,256]{2,0,1:T(8,128)(2,1)} %get-tuple-element.152), kind=kOutput, calls=%fused_computation.1 | convolution fusion | flops 543158272 | bytes 9977856 | tf_op jit(solution)/shard_map/cond/branch_1_fun/qhgd,khd->qhgk/dot_general | solution.py:115
  116.4 3.2 %fusion.7 = f32[512,2,4,128]{3,0,2,1:T(8,128)S(1)} fusion(f32[2,512,512,4]{2,1,3,0:T(8,128)S(1)} %get-tuple-element.264, pred[512,512]{0,1:T(8,128)(4,1)S(1)} %compare_and_fusion, bf16[512,2,256]{2,0,1:T(8,128)(2,1)} %get-tuple-element.152), kind=kOutput, calls=%fused_computation.7 | convolution fusion | flops 543162368 | bytes 11010048 | tf_op jit(solution)/shard_map/cond/branch_1_fun/qhgk,khd->qhgd/dot_general | solution.py:136
  119.6 7.5 %conditional.6 = ((f32[512,2,4,128]{3,0,2,1:T(8,128)S(1)}, f32[512,2,4]{0,2,1:T(4,128)S(1)})) conditional(s32[]{:T(128)} %bitcast.51, (f32[512,2,4,128]{3,0,2,1:T(8,128)S(1)}, f32[512,2,4]{0,2,1:T(4,128)S(1)}) %conditional.5, (s32[512]{0:T(512)S(1)}, s32[512]{0:T(512)S(1)}, s32[512]{0:T(512)S(1)}, s32[512]{0:T(512)S(1)}, s32[]{:T(128)}, ...), branch_computations={%region_5.6_spmd, %region_6.8_spmd} | conditional | flops 1088160768 | bytes 23416864 | solution.py:144
  120.2 3.1 %fusion.17 = (f32[512,2,4]{0,2,1:T(4,128)S(1)}, f32[2,512,512,4]{2,1,3,0:T(8,128)S(1)}) fusion(pred[512,512]{0,1:T(8,128)(4,1)S(1)} %compare_and_fusion.1, bf16[512,2,4,128]{3,0,2,1:T(8,128)(2,1)S(1)} %get-tuple-element.164, bf16[512,2,256]{2,0,1:T(8,128)(2,1)} %get-tuple-element.163), kind=kOutput, calls=%fused_computation.18 | convolution fusion | flops 543158272 | bytes 9977856 | tf_op jit(solution)/shard_map/cond/branch_1_fun/qhgd,khd->qhgk/dot_general | solution.py:115
  123.3 3.8 %bitcast_add_fusion = f32[512,2,4,128]{3,0,2,1:T(8,128)S(1)} fusion(f32[512,2,4,128]{3,0,2,1:T(8,128)S(1)} %get-tuple-element.154, f32[2,512,512,4]{2,1,3,0:T(8,128)S(1)} %get-tuple-element.266, pred[512,512]{0,1:T(8,128)(4,1)S(1)} %compare_and_fusion.1, bf16[512,2,256]{2,0,1:T(8,128)(2,1)} %get-tuple-element.163), kind=kOutput, calls=%fused_computation.24 | convolution fusion | flops 543686656 | bytes 13107200 | tf_op jit(solution)/shard_map/cond/branch_1_fun/qhgk,khd->qhgd/dot_general | solution.py:136
  129.0 28.7 %all_to_all.48 = bf16[512,8,128]{2,1,0:T(8,128)(2,1)S(1)} all-to-all(bf16[512,8,128]{2,1,0:T(8,128)(2,1)S(1)} %bitcast.167), channel_id=1, replica_groups=mesh['ctx'=8,'exp'=4] {'exp'}, dimensions={0} | all-to-all | bytes 2097152 | tf_op jit(solution)/shard_map/all_to_all | solution.py:157
  158.5 1.3 copy.65
  (49 shorter events, 15.9 us)
Async XLA Ops:
  0.0 33.0 %copy-start = (s32[128]{0:T(128)S(1)}, s32[128]{0:T(128)}, u32[]{:S(2)}) copy-start(s32[128]{0:T(128)} %param.18) | copy-start | bytes 1540
  0.0 50.6 %copy-start.1 = (s32[128]{0:T(128)S(1)}, s32[128]{0:T(128)}, u32[]{:S(2)}) copy-start(s32[128]{0:T(128)} %param.19) | copy-start | bytes 1540
  3.3 19.4 %all-to-all-start = ((bf16[128,8,256]{0,2,1:T(8,128)(2,1)}), bf16[128,8,256]{0,2,1:T(8,128)(2,1)S(1)}, u32[]{:S(2)}, u32[]{:S(2)}) async-start(bf16[128,8,256]{0,2,1:T(8,128)(2,1)} %pad_maximum_fusion), calls=%async_computation | async-start | bytes 1048576 | tf_op jit(solution)/shard_map/all_to_all | solution.py:47
  22.6 90.2 %all-to-all-start.1 = ((bf16[128,32,128]{2,0,1:T(8,128)(2,1)}), bf16[128,32,128]{2,0,1:T(8,128)(2,1)S(1)}, u32[]{:S(2)}, u32[]{:S(2)}) async-start(bf16[128,32,128]{2,0,1:T(8,128)(2,1)} %copy.60), calls=%async_computation.1 | async-start | bytes 2097152 | tf_op jit(solution)/shard_map/all_to_all | solution.py:46
  27.2 92.4 %collective-permute-start.8 = (bf16[512,2,256]{2,0,1:T(8,128)(2,1)}, bf16[512,2,256]{2,0,1:T(8,128)(2,1)}, u32[]{:S(2)}, u32[]{:S(2)}) collective-permute-start(bf16[512,2,256]{2,0,1:T(8,128)(2,1)} %bitcast.60), channel_id=1, source_target_pairs={{0,4},{4,8},{8,12},{12,16},{16,20},{20,24},{24,28},{1,5},{5,9},{9,... | collective-permute-start | bytes 1572872 | tf_op jit(solution)/shard_map/ppermute | solution.py:16
  29.1 98.0 %collective-permute-start.9 = (bf16[512,2,256]{2,0,1:T(8,128)(2,1)}, bf16[512,2,256]{2,0,1:T(8,128)(2,1)}, u32[]{:S(2)}, u32[]{:S(2)}) collective-permute-start(bf16[512,2,256]{2,0,1:T(8,128)(2,1)} %bitcast.60), channel_id=1, source_target_pairs={{0,8},{4,12},{8,16},{12,20},{16,24},{20,28},{1,9},{5,13},{9,17},{1... | collective-permute-start | bytes 1572872 | tf_op jit(solution)/shard_map/ppermute | solution.py:16
  30.4 96.8 %collective-permute-start.10 = (bf16[512,2,256]{2,0,1:T(8,128)(2,1)}, bf16[512,2,256]{2,0,1:T(8,128)(2,1)}, u32[]{:S(2)}, u32[]{:S(2)}) collective-permute-start(bf16[512,2,256]{2,0,1:T(8,128)(2,1)} %bitcast.60), channel_id=1, source_target_pairs={{0,12},{4,16},{8,20},{12,24},{16,28},{1,13},{5,17},{9,21},{13,25},... | collective-permute-start | bytes 1572872 | tf_op jit(solution)/shard_map/ppermute | solution.py:16
  31.7 95.7 %collective-permute-start.11 = (bf16[512,2,256]{2,0,1:T(8,128)(2,1)}, bf16[512,2,256]{2,0,1:T(8,128)(2,1)}, u32[]{:S(2)}, u32[]{:S(2)}) collective-permute-start(bf16[512,2,256]{2,0,1:T(8,128)(2,1)} %bitcast.60), channel_id=1, source_target_pairs={{0,16},{4,20},{8,24},{12,28},{1,17},{5,21},{9,25},{13,29},{2,18},{... | collective-permute-start | bytes 1572872 | tf_op jit(solution)/shard_map/ppermute | solution.py:16
  48.6 15.8 %collective-permute-start.6 = (s32[512]{0:T(512)S(1)}, s32[512]{0:T(512)S(1)}, u32[]{:S(2)}, u32[]{:S(2)}) collective-permute-start(s32[512]{0:T(512)S(1)} %bitcast.177), channel_id=1, source_target_pairs={{0,4},{4,8},{8,12},{12,16},{16,20},{20,24},{24,28},{1,5},{5,9},{9,... | collective-permute-start | bytes 6152 | tf_op jit(solution)/shard_map/ppermute | solution.py:16
  64.5 4.9 %collective-permute-start.7 = (s32[512]{0:T(512)S(1)}, s32[512]{0:T(512)S(1)}, u32[]{:S(2)}, u32[]{:S(2)}) collective-permute-start(s32[512]{0:T(512)S(1)} %bitcast.187), channel_id=1, source_target_pairs={{0,4},{4,8},{8,12},{12,16},{16,20},{20,24},{24,28},{1,5},{5,9},{9,... | collective-permute-start | bytes 6152 | tf_op jit(solution)/shard_map/ppermute | solution.py:16
  69.4 5.5 %collective-permute-start.4 = (s32[512]{0:T(512)S(1)}, s32[512]{0:T(512)S(1)}, u32[]{:S(2)}, u32[]{:S(2)}) collective-permute-start(s32[512]{0:T(512)S(1)} %bitcast.178), channel_id=1, source_target_pairs={{0,8},{4,12},{8,16},{12,20},{16,24},{20,28},{1,9},{5,13},{9,17},{1... | collective-permute-start | bytes 6152 | tf_op jit(solution)/shard_map/ppermute | solution.py:16
  74.9 5.9 %collective-permute-start.5 = (s32[512]{0:T(512)S(1)}, s32[512]{0:T(512)S(1)}, u32[]{:S(2)}, u32[]{:S(2)}) collective-permute-start(s32[512]{0:T(512)S(1)} %bitcast.188), channel_id=1, source_target_pairs={{0,8},{4,12},{8,16},{12,20},{16,24},{20,28},{1,9},{5,13},{9,17},{1... | collective-permute-start | bytes 6152 | tf_op jit(solution)/shard_map/ppermute | solution.py:16
  80.7 4.9 %collective-permute-start.2 = (s32[512]{0:T(512)S(1)}, s32[512]{0:T(512)S(1)}, u32[]{:S(2)}, u32[]{:S(2)}) collective-permute-start(s32[512]{0:T(512)S(1)} %bitcast.179), channel_id=1, source_target_pairs={{0,12},{4,16},{8,20},{12,24},{16,28},{1,13},{5,17},{9,21},{13,25},... | collective-permute-start | bytes 6152 | tf_op jit(solution)/shard_map/ppermute | solution.py:16
  85.6 4.9 %collective-permute-start.3 = (s32[512]{0:T(512)S(1)}, s32[512]{0:T(512)S(1)}, u32[]{:S(2)}, u32[]{:S(2)}) collective-permute-start(s32[512]{0:T(512)S(1)} %bitcast.189), channel_id=1, source_target_pairs={{0,12},{4,16},{8,20},{12,24},{16,28},{1,13},{5,17},{9,21},{13,25},... | collective-permute-start | bytes 6152 | tf_op jit(solution)/shard_map/ppermute | solution.py:16
  90.5 5.5 %collective-permute-start.1 = (s32[512]{0:T(512)S(1)}, s32[512]{0:T(512)S(1)}, u32[]{:S(2)}, u32[]{:S(2)}) collective-permute-start(s32[512]{0:T(512)S(1)} %bitcast.190), channel_id=1, source_target_pairs={{0,16},{4,20},{8,24},{12,28},{1,17},{5,21},{9,25},{13,29},{2,18},{... | collective-permute-start | bytes 6152 | tf_op jit(solution)/shard_map/ppermute | solution.py:16
  96.0 15.0 %collective-permute-start = (s32[512]{0:T(512)S(1)}, s32[512]{0:T(512)S(1)}, u32[]{:S(2)}, u32[]{:S(2)}) collective-permute-start(s32[512]{0:T(512)S(1)} %bitcast.181), channel_id=1, source_target_pairs={{0,16},{4,20},{8,24},{12,28},{1,17},{5,21},{9,25},{13,29},{2,18},{... | collective-permute-start | bytes 6152 | tf_op jit(solution)/shard_map/ppermute | solution.py:16
where the time goes:
time: 162 us; the launch traced here: 160 us
  blocking collectives  58.3 us (36%)
  waiting for transfers between devices  30.6 us (19%)
  starting transfers between devices  25.7 us (16%)
  local copies, waits for them, and re-layouts  15.6 us (10%)
  matrix products  13.2 us (8%)
  between operations  13 us (8%)
  other arithmetic  2.98 us (2%)
    all_to_all x1, blocking collectives, per_device(): lax.all_to_all(attended, 'exp', split_axis=0, concat_axis=1, tiled=True)  28.7 us
    ppermute x12, waiting for transfers between devices, shifted(): return lax.ppermute(block, axis, route)  19.6 us
    ppermute x12, starting transfers between devices, shifted(): return lax.ppermute(block, axis, route)  17.3 us
    all_gather x1, blocking collectives, per_device(): lax.all_gather(doc_ids, 'exp', axis=0, tiled=True)  15.6 us
    all_gather x1, blocking collectives, per_device(): lax.all_gather(span_ids, 'exp', axis=0, tiled=True)  13.9 us
    all_to_all x1, waiting for transfers between devices, per_device(): lax.all_to_all(paired, 'exp', split_axis=1, concat_axis=0, tiled=True)  11 us
    dot_general x2, matrix products, compute(): jnp.einsum('qhgk,khd->qhgd', weights.astype(jnp.bfloat16), kv_tile[:, :,...  7.01 us
    dot_general x2, matrix products, compute(): jnp.einsum('qhgd,khd->qhgk', query_tile, kv_tile[:, :, :HEAD_SIZE], prefe...  6.2 us
  transfers between devices with their start and end apart: 14, of which 7 were waited for; matrix products, arithmetic and copies ran while one was open for 16% of the time, Pallas kernels for 0%

commit v1 on v0

--- a/solution.py
+++ b/solution.py
@@ -1,6 +1,10 @@
+import math
+
 import jax
 import jax.numpy as jnp
 from jax import lax
+from jax.experimental import pallas as pl
+from jax.experimental.pallas import tpu as pltpu
 from jax.sharding import PartitionSpec as P
 
 QUERY_HEADS = 32
@@ -8,6 +12,10 @@
 HEAD_SIZE = 128
 SPAN = 8192
 DOC_LEN = 2048
+PACKED_TOKENS = 4096
+DOC_TOP = 1024
+GROUP = QUERY_HEADS // KEY_VALUE_HEADS
+MESH = pl.DeviceIdType.MESH
 
 
 def shifted(block, axis, distance):
@@ -22,7 +30,7 @@
     return (widened * factor).astype(jnp.bfloat16)
 
 
-def per_device(queries, keys, values, doc_ids, span_ids):
+def general(queries, keys, values, doc_ids, span_ids):
     expanded_size = lax.axis_size("exp")
     ctx_size = lax.axis_size("ctx")
     shard_rows = queries.shape[0]
@@ -158,6 +166,201 @@
     return returned.reshape(shard_rows, QUERY_HEADS * HEAD_SIZE)
 
 
+def unit_tile(tile):
+    widened = tile.astype(jnp.float32)
+    factor = lax.rsqrt(jnp.mean(widened * widened, axis=-1, keepdims=True) + 1e-06)
+    return (widened * factor).astype(jnp.bfloat16)
+
+
+def relay_kernel(
+    blocks, lanes, q_ref, k_ref, v_ref, id_ref, out_ref,
+    q_raw, q_unit, k_all, v_all, id_all, own_col, acc,
+    own_sem, recv_sem, send_sem,
+):
+    rows = k_ref.shape[0]
+    ctx = lax.axis_index("ctx")
+    z = lax.axis_index("exp")
+    even = ctx % 2 == 0
+    inputs = (k_ref, v_ref, id_ref)
+    slots = (k_all, v_all, id_all)
+
+    barrier = pltpu.get_barrier_semaphore()
+    neighbours = [
+        (z > 0, (ctx, z - 1)), (z < lanes - 1, (ctx, z + 1)),
+        (ctx > 0, (ctx - 1, z)), (ctx < blocks - 1, (ctx + 1, z)),
+        (ctx > 1, (ctx - 2, z)), (ctx < blocks - 2, (ctx + 2, z)),
+    ]
+    for present, device in neighbours:
+        @pl.when(present)
+        def _(device=device):
+            pl.semaphore_signal(barrier, inc=1, device_id=device, device_id_type=MESH)
+    pl.semaphore_wait(barrier, sum(present.astype(jnp.int32) for present, _ in neighbours))
+
+    def send(way, b, zp, device, to_b, own, finish):
+        for part in range(3):
+            source = inputs[part] if own else slots[part].at[b * lanes + zp]
+            copy = pltpu.make_async_remote_copy(
+                src_ref=source,
+                dst_ref=slots[part].at[to_b * lanes + zp],
+                send_sem=send_sem.at[way, b * lanes + zp, part],
+                recv_sem=recv_sem.at[to_b * lanes + zp, part],
+                device_id=device,
+                device_id_type=MESH,
+            )
+            if finish:
+                copy.wait_send()
+            else:
+                copy.start()
+
+    def forward(b, zp, own=False, finish=False):
+        routes = []
+        if b == 0:
+            routes.append((0, (zp <= z) & (z < lanes - 1), (ctx, z + 1), 0))
+        if b <= 1:
+            routes.append((1, even & (z > 0) & (zp >= z), (ctx, z - 1), b))
+        if b == 0:
+            routes.append((2, even | ((zp <= z) & (ctx < blocks - 1)), (ctx + 1, z), 1))
+            routes.append((3, even & (zp >= z) & (ctx < blocks - 2), (ctx + 2, z), 2))
+        if b == 1:
+            routes.append((2, even & (zp >= z), (ctx + 1, z), 2))
+        for way, taken, device, to_b in routes:
+            @pl.when(taken)
+            def _(way=way, device=device, to_b=to_b):
+                send(way, b, zp, device, to_b, own, finish)
+
+    forward(0, z, own=True)
+
+    own_copies = [
+        pltpu.make_async_copy(inputs[part], slots[part].at[z], own_sem.at[part]) for part in range(3)
+    ]
+    q_copy = pltpu.make_async_copy(q_ref, q_raw, own_sem.at[3])
+    for copy in [q_copy] + own_copies:
+        copy.start()
+    acc[...] = jnp.zeros_like(acc)
+    q_copy.wait()
+
+    @pl.loop(0, KEY_VALUE_HEADS)
+    def _(g):
+        for j in range(GROUP):
+            column = pl.multiple_of((g * GROUP + j) * HEAD_SIZE, HEAD_SIZE)
+            q_unit[g, pl.ds(j * rows, rows), :] = unit_tile(q_raw[:, pl.ds(column, HEAD_SIZE)])
+
+    for copy in own_copies:
+        copy.wait()
+    own_row = id_all[z][0:1, :]
+    own_col[...] = jnp.broadcast_to(own_row, (rows, rows)).T
+
+    scale = math.log2(math.e) * HEAD_SIZE ** (-0.5)
+
+    def attend(slot, own=False):
+        same = own_col[...] == jnp.broadcast_to(id_all[slot][0:1, :], (rows, rows))
+        if own:
+            same = same & (
+                lax.broadcasted_iota(jnp.int32, (rows, rows), 1)
+                <= lax.broadcasted_iota(jnp.int32, (rows, rows), 0)
+            )
+        same = jnp.concatenate([same.astype(jnp.float32)] * GROUP, axis=0) > 0.5
+        ones = jnp.ones((rows, HEAD_SIZE), jnp.bfloat16)
+
+        @pl.loop(0, KEY_VALUE_HEADS)
+        def _(g):
+            column = pl.ds(pl.multiple_of(g * HEAD_SIZE, HEAD_SIZE), HEAD_SIZE)
+            key = unit_tile(k_all[slot, :, column])
+            scores = lax.dot_general(
+                q_unit[g], key, (((1,), (1,)), ((), ())), preferred_element_type=jnp.float32
+            )
+            weights = jnp.where(same, jnp.exp2(scores * scale), 0.0).astype(jnp.bfloat16)
+            value = jnp.concatenate([v_all[slot, :, column], ones], axis=1)
+            acc[g] += jnp.dot(weights, value, preferred_element_type=jnp.float32)
+
+    attend(z, own=True)
+
+    def receive(b, zp, needed):
+        slot = b * lanes + zp
+        for part in range(3):
+            pltpu.make_async_remote_copy(
+                src_ref=slots[part].at[slot],
+                dst_ref=slots[part].at[slot],
+                send_sem=send_sem.at[0, slot, part],
+                recv_sem=recv_sem.at[slot, part],
+                device_id=(ctx, z),
+                device_id_type=MESH,
+            ).wait_recv()
+        forward(b, zp)
+        if needed:
+            attend(slot)
+
+    @pl.loop(0, lanes)
+    def _(d):
+        for b, zp, valid, needed in (
+            (0, z - d - 1, z - d - 1 >= 0, True),
+            (0, z + d + 1, even & (z + d + 1 < lanes), False),
+            (1, z + d, (ctx > 0) & (z + d < lanes), True),
+            (1, z - d, (ctx > 0) & (z - d >= 0) & (d > 0), True),
+            (2, z + d, (ctx > 1) & (z + d < lanes), True),
+        ):
+            @pl.when(valid)
+            def _(b=b, zp=zp, needed=needed):
+                receive(b, zp, needed)
+
+    @pl.loop(0, KEY_VALUE_HEADS)
+    def _(g):
+        for j in range(GROUP):
+            column = pl.multiple_of((g * GROUP + j) * HEAD_SIZE, HEAD_SIZE)
+            part = acc[g, pl.ds(j * rows, rows), :]
+            out_ref[:, pl.ds(column, HEAD_SIZE)] = (
+                part[:, :HEAD_SIZE] / part[:, HEAD_SIZE:]
+            ).astype(jnp.bfloat16)
+
+    @pl.loop(0, lanes)
+    def _(zp):
+        @pl.when((zp <= z) | even)
+        def _():
+            forward(0, zp, finish=True)
+
+        @pl.when(ctx > 0)
+        def _():
+            forward(1, zp, finish=True)
+
+
+def relayed(queries, keys, values, doc_ids, span_ids):
+    lanes = lax.axis_size("exp")
+    blocks = lax.axis_size("ctx")
+    rows = queries.shape[0]
+    codes = jnp.broadcast_to((doc_ids * 65536 + span_ids)[None, :], (8, rows))
+    count = 3 * lanes
+    bf16, f32 = jnp.bfloat16, jnp.float32
+    return pl.pallas_call(
+        lambda *refs: relay_kernel(blocks, lanes, *refs),
+        out_shape=jax.ShapeDtypeStruct(queries.shape, bf16),
+        in_specs=[pl.BlockSpec(memory_space=pl.ANY)] * 4,
+        out_specs=pl.BlockSpec(memory_space=pltpu.VMEM),
+        scratch_shapes=[
+            pltpu.VMEM(queries.shape, bf16),
+            pltpu.VMEM((KEY_VALUE_HEADS, GROUP * rows, HEAD_SIZE), bf16),
+            pltpu.VMEM((count,) + keys.shape, bf16),
+            pltpu.VMEM((count,) + values.shape, bf16),
+            pltpu.VMEM((count, 8, rows), jnp.int32),
+            pltpu.VMEM((rows, rows), jnp.int32),
+            pltpu.VMEM((KEY_VALUE_HEADS, GROUP * rows, 2 * HEAD_SIZE), f32),
+            pltpu.SemaphoreType.DMA((4,)),
+            pltpu.SemaphoreType.DMA((count, 3)),
+            pltpu.SemaphoreType.DMA((4, count, 3)),
+        ],
+        compiler_params=pltpu.CompilerParams(collective_id=0, has_side_effects=True),
+    )(queries, keys, values, codes)
+
+
+def per_device(queries, keys, values, doc_ids, span_ids):
+    lanes, blocks = lax.axis_size("exp"), lax.axis_size("ctx")
+    rows = queries.shape[0]
+    tokens = rows * lanes * blocks
+    reach = min(SPAN, DOC_LEN if tokens > PACKED_TOKENS else DOC_TOP)
+    if reach <= 2 * lanes * rows and blocks % 2 == 0 and lanes <= 8 and rows % 128 == 0:
+        return relayed(queries, keys, values, doc_ids, span_ids)
+    return general(queries, keys, values, doc_ids, span_ids)
+
+
 def solution(mesh):
     in_specs = (
         P(("ctx", "exp"), None),

time: 162 us -> 68.4 us (0.42)
  Pallas kernels: 0 us -> 64.1 us
  blocking collectives: 58.3 us -> 0 us
  waiting for transfers between devices: 30.6 us -> 0 us
  starting transfers between devices: 25.7 us -> 0 us
  matrix products: 13.2 us -> 0 us
  between operations: 13 us -> 0.01 us
  local copies, waits for them, and re-layouts: 15.6 us -> 2.88 us
  other arithmetic: 2.98 us -> 0.67 us
    pallas_call x0 -> x1, Pallas kernels: none -> 64.1 us  [relayed(): pl.pallas_call(lambda *refs: relay_kernel(blocks, lanes, *refs), out_shap...]
    all_gather x2 -> x0, blocking collectives: 29.5 us -> none  [the longest x1 15.6 us: per_device(): lax.all_gather(doc_ids, 'exp', axis=0, tiled=True)]
    all_to_all x1 -> x0, blocking collectives: 28.7 us -> none  [per_device(): lax.all_to_all(attended, 'exp', split_axis=0, concat_axis=1, tiled=True)]
    ppermute x12 -> x0, waiting for transfers between devices: 19.6 us -> none  [shifted(): return lax.ppermute(block, axis, route)]
    ppermute x12 -> x0, starting transfers between devices: 17.3 us -> none  [shifted(): return lax.ppermute(block, axis, route)]
    dot_general x4 -> x0, matrix products: 13.2 us -> none  [the longest x2 7.01 us: compute(): jnp.einsum('qhgk,khd->qhgd', weights.astype(jnp.bfloat16), kv_tile[:, :,...]
    all_to_all x2 -> x0, waiting for transfers between devices: 11 us -> none  [the longest x1 11 us: per_device(): lax.all_to_all(paired, 'exp', split_axis=1, concat_axis=0, tiled=True)]
    all_to_all x2 -> x0, starting transfers between devices: 8.39 us -> none  [the longest x1 4.87 us: per_device(): lax.all_to_all(paired, 'exp', split_axis=1, concat_axis=0, tiled=True)]
  transfers between devices with their start and end apart: 14 -> 0, of which waited for: 7 -> 0; matrix products, arithmetic and copies ran while one was open for 16% -> 0% of each run, Pallas kernels for 0% -> 0%
where the time goes in v1:
time: 68.4 us; the launch traced here: 67.7 us
  Pallas kernels  64.1 us (94%)
  local copies, waits for them, and re-layouts  2.88 us (4%)
    pallas_call x1, Pallas kernels, relayed(): pl.pallas_call(lambda *refs: relay_kernel(blocks, lanes, *refs), out_shap...  64.1 us
    unnamed x1, local copies, waits for them, and re-layouts  2.29 us

profile of v1, /device:TPU:6, one launch (start us, length us, event | category | flops | bytes accessed | tf_op | source)
XLA Modules:
  0.0 67.7 jit_solution(7864845193369942424)
XLA Ops:
  0.0 0.7 multiply_add_fusion
  0.7 0.6 broadcast_in_dim.2.refs_3_
  1.3 64.1 %shard_map.55 = bf16[128,4096]{1,0:T(8,128)(2,1)} custom-call(bf16[128,4096]{1,0:T(8,128)(2,1)} %refs_0_.1, bf16[128,1024]{1,0:T(8,128)(2,1)} %refs_1_.1, bf16[128,1024]{1,0:T(8,128)(2,1)} %refs_2_.1, s32[8,128]{1,0:T(8,128)} %broadcast_in_dim.2.refs_3_), custom_call_target="tpu_custom_call" | custom-call | tf_op jit(solution)/shard_map/pallas_call | solution.py:333
  65.4 2.3 %copy.7 = bf16[128,4096]{1,0:T(8,128)(2,1)} copy(bf16[128,4096]{1,0:T(8,128)(2,1)} %shard_map.55) | data formatting | bytes 2097152

commit v2 on v1

--- a/solution.py
+++ b/solution.py
@@ -173,7 +173,7 @@
 
 
 def relay_kernel(
-    blocks, lanes, q_ref, k_ref, v_ref, id_ref, out_ref,
+    blocks, lanes, q_ref, k_ref, v_ref, doc_ref, span_ref, out_ref,
     q_raw, q_unit, k_all, v_all, id_all, own_col, acc,
     own_sem, recv_sem, send_sem,
 ):
@@ -181,8 +181,8 @@
     ctx = lax.axis_index("ctx")
     z = lax.axis_index("exp")
     even = ctx % 2 == 0
-    inputs = (k_ref, v_ref, id_ref)
     slots = (k_all, v_all, id_all)
+    inputs = (k_ref, v_ref, id_all.at[z])
 
     barrier = pltpu.get_barrier_semaphore()
     neighbours = [
@@ -196,50 +196,56 @@
             pl.semaphore_signal(barrier, inc=1, device_id=device, device_id_type=MESH)
     pl.semaphore_wait(barrier, sum(present.astype(jnp.int32) for present, _ in neighbours))
 
-    def send(way, b, zp, device, to_b, own, finish):
-        for part in range(3):
-            source = inputs[part] if own else slots[part].at[b * lanes + zp]
-            copy = pltpu.make_async_remote_copy(
-                src_ref=source,
-                dst_ref=slots[part].at[to_b * lanes + zp],
-                send_sem=send_sem.at[way, b * lanes + zp, part],
-                recv_sem=recv_sem.at[to_b * lanes + zp, part],
-                device_id=device,
-                device_id_type=MESH,
-            )
-            if finish:
-                copy.wait_send()
-            else:
-                copy.start()
-
-    def forward(b, zp, own=False, finish=False):
+    def send(way, b, zp, device, to_b, part, own, finish):
+        copy = pltpu.make_async_remote_copy(
+            src_ref=inputs[part] if own else slots[part].at[b * lanes + zp],
+            dst_ref=slots[part].at[to_b * lanes + zp],
+            send_sem=send_sem.at[way, b * lanes + zp, part],
+            recv_sem=recv_sem.at[to_b * lanes + zp, part],
+            device_id=device,
+            device_id_type=MESH,
+        )
+        if finish:
+            copy.wait_send()
+        else:
+            copy.start()
+
+    def forward(b, zp, parts=(0, 1, 2), ways=(0, 1, 2, 3), own=False, finish=False):
         routes = []
-        if b == 0:
-            routes.append((0, (zp <= z) & (z < lanes - 1), (ctx, z + 1), 0))
         if b <= 1:
             routes.append((1, even & (z > 0) & (zp >= z), (ctx, z - 1), b))
         if b == 0:
             routes.append((2, even | ((zp <= z) & (ctx < blocks - 1)), (ctx + 1, z), 1))
+            routes.append((0, (zp <= z) & (z < lanes - 1), (ctx, z + 1), 0))
             routes.append((3, even & (zp >= z) & (ctx < blocks - 2), (ctx + 2, z), 2))
         if b == 1:
             routes.append((2, even & (zp >= z), (ctx + 1, z), 2))
         for way, taken, device, to_b in routes:
-            @pl.when(taken)
-            def _(way=way, device=device, to_b=to_b):
-                send(way, b, zp, device, to_b, own, finish)
-
-    forward(0, z, own=True)
-
+            if way in ways:
+                @pl.when(taken)
+                def _(way=way, device=device, to_b=to_b):
+                    for part in parts:
+                        send(way, b, zp, device, to_b, part, own, finish)
+
+    forward(0, z, parts=(0, 1), ways=(0, 1, 2), own=True)
+
+    id_copies = [
+        pltpu.make_async_copy(ref, id_all.at[z, pl.ds(row, 1)], own_sem.at[row])
+        for row, ref in enumerate((doc_ref, span_ref))
+    ]
     own_copies = [
-        pltpu.make_async_copy(inputs[part], slots[part].at[z], own_sem.at[part]) for part in range(3)
-    ]
-    q_copy = pltpu.make_async_copy(q_ref, q_raw, own_sem.at[3])
-    for copy in [q_copy] + own_copies:
+        pltpu.make_async_copy(inputs[part], slots[part].at[z], own_sem.at[2 + part]) for part in range(2)
+    ]
+    q_copy = pltpu.make_async_copy(q_ref, q_raw, own_sem.at[4])
+    for copy in id_copies + [q_copy] + own_copies:
         copy.start()
+    for copy in id_copies:
+        copy.wait()
+    forward(0, z, parts=(2,), ways=(0, 1, 2), own=True)
     acc[...] = jnp.zeros_like(acc)
     q_copy.wait()
 
-    @pl.loop(0, KEY_VALUE_HEADS)
+    @pl.loop(0, KEY_VALUE_HEADS, unroll=4)
     def _(g):
         for j in range(GROUP):
             column = pl.multiple_of((g * GROUP + j) * HEAD_SIZE, HEAD_SIZE)
@@ -247,33 +253,41 @@
 
     for copy in own_copies:
         copy.wait()
-    own_row = id_all[z][0:1, :]
-    own_col[...] = jnp.broadcast_to(own_row, (rows, rows)).T
+
+    def codes(slot):
+        ids = id_all[slot]
+        return jnp.broadcast_to(ids[0:1, :] * 65536 + ids[1:2, :], (rows, rows))
+
+    own_col[...] = codes(z).T
 
     scale = math.log2(math.e) * HEAD_SIZE ** (-0.5)
 
     def attend(slot, own=False):
-        same = own_col[...] == jnp.broadcast_to(id_all[slot][0:1, :], (rows, rows))
+        same = own_col[...] == codes(slot)
         if own:
             same = same & (
                 lax.broadcasted_iota(jnp.int32, (rows, rows), 1)
                 <= lax.broadcasted_iota(jnp.int32, (rows, rows), 0)
             )
-        same = jnp.concatenate([same.astype(jnp.float32)] * GROUP, axis=0) > 0.5
+        kept = same.astype(jnp.float32).astype(jnp.bfloat16)
         ones = jnp.ones((rows, HEAD_SIZE), jnp.bfloat16)
 
-        @pl.loop(0, KEY_VALUE_HEADS)
+        @pl.loop(0, KEY_VALUE_HEADS, unroll=KEY_VALUE_HEADS)
         def _(g):
             column = pl.ds(pl.multiple_of(g * HEAD_SIZE, HEAD_SIZE), HEAD_SIZE)
             key = unit_tile(k_all[slot, :, column])
             scores = lax.dot_general(
                 q_unit[g], key, (((1,), (1,)), ((), ())), preferred_element_type=jnp.float32
             )
-            weights = jnp.where(same, jnp.exp2(scores * scale), 0.0).astype(jnp.bfloat16)
+            weights = jnp.exp2(scores * scale).astype(jnp.bfloat16)
+            weights = jnp.concatenate(
+                [weights[j * rows : (j + 1) * rows] * kept for j in range(GROUP)], axis=0
+            )
             value = jnp.concatenate([v_all[slot, :, column], ones], axis=1)
             acc[g] += jnp.dot(weights, value, preferred_element_type=jnp.float32)
 
     attend(z, own=True)
+    forward(0, z, ways=(3,), own=True)
 
     def receive(b, zp, needed):
         slot = b * lanes + zp
@@ -286,16 +300,16 @@
                 device_id=(ctx, z),
                 device_id_type=MESH,
             ).wait_recv()
-        forward(b, zp)
+            forward(b, zp, parts=(part,))
         if needed:
             attend(slot)
 
     @pl.loop(0, lanes)
     def _(d):
         for b, zp, valid, needed in (
-            (0, z - d - 1, z - d - 1 >= 0, True),
             (0, z + d + 1, even & (z + d + 1 < lanes), False),
             (1, z + d, (ctx > 0) & (z + d < lanes), True),
+            (0, z - d - 1, z - d - 1 >= 0, True),
             (1, z - d, (ctx > 0) & (z - d >= 0) & (d > 0), True),
             (2, z + d, (ctx > 1) & (z + d < lanes), True),
         ):
@@ -303,7 +317,7 @@
             def _(b=b, zp=zp, needed=needed):
                 receive(b, zp, needed)
 
-    @pl.loop(0, KEY_VALUE_HEADS)
+    @pl.loop(0, KEY_VALUE_HEADS, unroll=4)
     def _(g):
         for j in range(GROUP):
             column = pl.multiple_of((g * GROUP + j) * HEAD_SIZE, HEAD_SIZE)
@@ -327,28 +341,27 @@
     lanes = lax.axis_size("exp")
     blocks = lax.axis_size("ctx")
     rows = queries.shape[0]
-    codes = jnp.broadcast_to((doc_ids * 65536 + span_ids)[None, :], (8, rows))
     count = 3 * lanes
     bf16, f32 = jnp.bfloat16, jnp.float32
     return pl.pallas_call(
         lambda *refs: relay_kernel(blocks, lanes, *refs),
         out_shape=jax.ShapeDtypeStruct(queries.shape, bf16),
-        in_specs=[pl.BlockSpec(memory_space=pl.ANY)] * 4,
+        in_specs=[pl.BlockSpec(memory_space=pl.ANY)] * 5,
         out_specs=pl.BlockSpec(memory_space=pltpu.VMEM),
         scratch_shapes=[
             pltpu.VMEM(queries.shape, bf16),
             pltpu.VMEM((KEY_VALUE_HEADS, GROUP * rows, HEAD_SIZE), bf16),
             pltpu.VMEM((count,) + keys.shape, bf16),
             pltpu.VMEM((count,) + values.shape, bf16),
-            pltpu.VMEM((count, 8, rows), jnp.int32),
+            pltpu.VMEM((count, 2, rows), jnp.int32),
             pltpu.VMEM((rows, rows), jnp.int32),
             pltpu.VMEM((KEY_VALUE_HEADS, GROUP * rows, 2 * HEAD_SIZE), f32),
-            pltpu.SemaphoreType.DMA((4,)),
+            pltpu.SemaphoreType.DMA((5,)),
             pltpu.SemaphoreType.DMA((count, 3)),
             pltpu.SemaphoreType.DMA((4, count, 3)),
         ],
         compiler_params=pltpu.CompilerParams(collective_id=0, has_side_effects=True),
-    )(queries, keys, values, codes)
+    )(queries, keys, values, doc_ids[None, :], span_ids[None, :])
 
 
 def per_device(queries, keys, values, doc_ids, span_ids):

time: 68.4 us -> 49.8 us (0.73)
  the two profiles are of different devices: /device:TPU:6 before, /device:TPU:5 now
where the time goes in v2:
time: 49.8 us; the launch traced here: 49.6 us
  Pallas kernels  47.3 us (95%)
  local copies, waits for them, and re-layouts  2.29 us (5%)
    pallas_call x1, Pallas kernels, relayed(): pl.pallas_call(lambda *refs: relay_kernel(blocks, lanes, *refs), out_shap...  47.3 us
    unnamed x1, local copies, waits for them, and re-layouts  2.29 us

profile of v2, /device:TPU:5, one launch (start us, length us, event | category | flops | bytes accessed | tf_op | source)
XLA Modules:
  0.0 49.6 jit_solution(17565824982046531273)
XLA Ops:
  0.0 47.3 %shard_map.55 = bf16[128,4096]{1,0:T(8,128)(2,1)} custom-call(bf16[128,4096]{1,0:T(8,128)(2,1)} %refs_0_.1, bf16[128,1024]{1,0:T(8,128)(2,1)} %refs_1_.1, bf16[128,1024]{1,0:T(8,128)(2,1)} %refs_2_.1, s32[1,128]{1,0:T(1,128)} %bitcast.2, s32[1,128]{1,0:T(1,128)} %bitcast.3), custom_call_target="tpu_custom_call" | custom-call | tf_op jit(solution)/shard_map/pallas_call | solution.py:346
  47.3 2.3 %copy.7 = bf16[128,4096]{1,0:T(8,128)(2,1)} copy(bf16[128,4096]{1,0:T(8,128)(2,1)} %shard_map.55) | data formatting | bytes 2097152

commit v3 on v2

--- a/solution.py
+++ b/solution.py
@@ -210,7 +210,7 @@
         else:
             copy.start()
 
-    def forward(b, zp, parts=(0, 1, 2), ways=(0, 1, 2, 3), own=False, finish=False):
+    def forward(b, zp, parts=(0, 1, 2), ways=(0, 1, 2, 3), also=True, own=False, finish=False):
         routes = []
         if b <= 1:
             routes.append((1, even & (z > 0) & (zp >= z), (ctx, z - 1), b))
@@ -222,12 +222,13 @@
             routes.append((2, even & (zp >= z), (ctx + 1, z), 2))
         for way, taken, device, to_b in routes:
             if way in ways:
-                @pl.when(taken)
+                @pl.when(taken & also)
                 def _(way=way, device=device, to_b=to_b):
                     for part in parts:
                         send(way, b, zp, device, to_b, part, own, finish)
 
-    forward(0, z, parts=(0, 1), ways=(0, 1, 2), own=True)
+    forward(0, z, parts=(0, 1), ways=(1, 2), own=True)
+    forward(0, z, parts=(0, 1), ways=(0,), also=~even, own=True)
 
     id_copies = [
         pltpu.make_async_copy(ref, id_all.at[z, pl.ds(row, 1)], own_sem.at[row])
@@ -241,7 +242,8 @@
         copy.start()
     for copy in id_copies:
         copy.wait()
-    forward(0, z, parts=(2,), ways=(0, 1, 2), own=True)
+    forward(0, z, parts=(2,), ways=(1, 2), own=True)
+    forward(0, z, parts=(2,), ways=(0,), also=~even, own=True)
     acc[...] = jnp.zeros_like(acc)
     q_copy.wait()
 
@@ -287,6 +289,7 @@
             acc[g] += jnp.dot(weights, value, preferred_element_type=jnp.float32)
 
     attend(z, own=True)
+    forward(0, z, ways=(0,), also=even, own=True)
     forward(0, z, ways=(3,), own=True)
 
     def receive(b, zp, needed):
@@ -304,14 +307,17 @@
         if needed:
             attend(slot)
 
-    @pl.loop(0, lanes)
+    late = (z > 0).astype(jnp.int32)
+
+    @pl.loop(0, lanes + 1)
     def _(d):
+        e = d - late
         for b, zp, valid, needed in (
             (0, z + d + 1, even & (z + d + 1 < lanes), False),
             (1, z + d, (ctx > 0) & (z + d < lanes), True),
             (0, z - d - 1, z - d - 1 >= 0, True),
-            (1, z - d, (ctx > 0) & (z - d >= 0) & (d > 0), True),
-            (2, z + d, (ctx > 1) & (z + d < lanes), True),
+            (1, z - e, (ctx > 0) & (z - e >= 0) & (e > 0), True),
+            (2, z + e, (ctx > 1) & (z + e < lanes) & (e >= 0), True),
         ):
             @pl.when(valid)
             def _(b=b, zp=zp, needed=needed):
@@ -345,8 +351,8 @@
     bf16, f32 = jnp.bfloat16, jnp.float32
     return pl.pallas_call(
         lambda *refs: relay_kernel(blocks, lanes, *refs),
-        out_shape=jax.ShapeDtypeStruct(queries.shape, bf16),
-        in_specs=[pl.BlockSpec(memory_space=pl.ANY)] * 5,
+        out_shape=pltpu.VMEM(queries.shape, bf16),
+        in_specs=[pl.BlockSpec(memory_space=pltpu.HBM)] * 5,
         out_specs=pl.BlockSpec(memory_space=pltpu.VMEM),
         scratch_shapes=[
             pltpu.VMEM(queries.shape, bf16),
@@ -360,7 +366,7 @@
             pltpu.SemaphoreType.DMA((count, 3)),
             pltpu.SemaphoreType.DMA((4, count, 3)),
         ],
-        compiler_params=pltpu.CompilerParams(collective_id=0, has_side_effects=True),
+        compiler_params=pltpu.CompilerParams(collective_id=0, has_side_effects=True, vmem_limit_bytes=60 << 20),
     )(queries, keys, values, doc_ids[None, :], span_ids[None, :])
 
 

time: 49.8 us -> 46.4 us (0.932)
  the two profiles are of different devices: /device:TPU:5 before, /device:TPU:28 now
where the time goes in v3:
time: 46.4 us; the launch traced here: 46.2 us
  Pallas kernels  45.2 us (97%)
  local copies, waits for them, and re-layouts  0.97 us (2%)
    pallas_call x1, Pallas kernels, relayed(): pl.pallas_call(lambda *refs: relay_kernel(blocks, lanes, *refs), out_shap...  45.2 us
    unnamed x1, local copies, waits for them, and re-layouts  0.97 us

profile of v3, /device:TPU:28, one launch (start us, length us, event | category | flops | bytes accessed | tf_op | source)
XLA Modules:
  0.0 46.2 jit_solution(4412540565349919503)
XLA Ops:
  0.0 45.2 %shard_map.55 = bf16[128,4096]{1,0:T(8,128)(2,1)S(1)} custom-call(bf16[128,4096]{1,0:T(8,128)(2,1)} %refs_0_.1, bf16[128,1024]{1,0:T(8,128)(2,1)} %refs_1_.1, bf16[128,1024]{1,0:T(8,128)(2,1)} %refs_2_.1, s32[1,128]{1,0:T(1,128)} %bitcast.2, s32[1,128]{1,0:T(1,128)} %bitcast.3), custom_call_target="tpu_custom_call" | custom-call | tf_op jit(solution)/shard_map/pallas_call | solution.py:352
  45.3 1.0 %copy.7 = bf16[128,4096]{1,0:T(8,128)(2,1)} copy(bf16[128,4096]{1,0:T(8,128)(2,1)S(1)} %shard_map.55) | data formatting | bytes 2097152

commit v4 on v3

--- a/solution.py
+++ b/solution.py
@@ -307,17 +307,17 @@
         if needed:
             attend(slot)
 
-    late = (z > 0).astype(jnp.int32)
-
-    @pl.loop(0, lanes + 1)
+    late = 2 * ((z > 0) & (z < lanes - 1)).astype(jnp.int32)
+
+    @pl.loop(0, lanes + 2)
     def _(d):
         e = d - late
         for b, zp, valid, needed in (
+            (1, z - e, (ctx > 0) & (z - e >= 0) & (e > 0), True),
+            (2, z + e, (ctx > 1) & (z + e < lanes) & (e >= 0), True),
             (0, z + d + 1, even & (z + d + 1 < lanes), False),
             (1, z + d, (ctx > 0) & (z + d < lanes), True),
             (0, z - d - 1, z - d - 1 >= 0, True),
-            (1, z - e, (ctx > 0) & (z - e >= 0) & (e > 0), True),
-            (2, z + e, (ctx > 1) & (z + e < lanes) & (e >= 0), True),
         ):
             @pl.when(valid)
             def _(b=b, zp=zp, needed=needed):

time: 46.4 us -> 49.8 us (1.073)
  the two profiles are of different devices: /device:TPU:28 before, /device:TPU:30 now
where the time goes in v4:
time: 49.8 us; the launch traced here: 49.7 us
  Pallas kernels  48.7 us (98%)
  local copies, waits for them, and re-layouts  0.97 us (2%)
    pallas_call x1, Pallas kernels, relayed(): pl.pallas_call(lambda *refs: relay_kernel(blocks, lanes, *refs), out_shap...  48.7 us

profile of v4, /device:TPU:30, one launch (start us, length us, event | category | flops | bytes accessed | tf_op | source)
XLA Modules:
  0.0 49.7 jit_solution(8060854871219296129)
XLA Ops:
  0.0 48.7 %shard_map.55 = bf16[128,4096]{1,0:T(8,128)(2,1)S(1)} custom-call(bf16[128,4096]{1,0:T(8,128)(2,1)} %refs_0_.1, bf16[128,1024]{1,0:T(8,128)(2,1)} %refs_1_.1, bf16[128,1024]{1,0:T(8,128)(2,1)} %refs_2_.1, s32[1,128]{1,0:T(1,128)} %bitcast.2, s32[1,128]{1,0:T(1,128)} %bitcast.3), custom_call_target="tpu_custom_call" | custom-call | tf_op jit(solution)/shard_map/pallas_call | solution.py:352
  48.7 1.0 %copy.7 = bf16[128,4096]{1,0:T(8,128)(2,1)} copy(bf16[128,4096]{1,0:T(8,128)(2,1)S(1)} %shard_map.55) | data formatting | bytes 2097152
